TPU v7x, 32 devices: a whole 2x2x4 slice. The times are simulated.
32 devices in a mesh: dp: 16 (over z, y, core), mp: 2 (over x).
Axes of the slice: x: 2, y: 2, z: 4, core: 2. Of those that a mesh axis runs over, the one named last changes fastest.
Arguments:
- patch_counts: int32 [128], P('dp'), may hold values from 100 to 240, as said below
- tokens: bfloat16 [128, 280, 768], P('dp'), may hold values from -6 to 6
- cotangent: bfloat16 [128, 280, 768], P('dp'), may hold values from -6 to 6
- attn_gain: float32 [768], P('dp'), may hold values from 0.1 to 1.9
- attn_shift: float32 [768], P('dp'), may hold values from -1.75 to 1.75
- w_qkv: float32 [768, 3, 768], P('dp', None, 'mp'), may hold values from -0.21875 to 0.21875
- b_qv: float32 [2, 768], P(None, 'mp'), may hold values from -3 to 3
- w_proj: float32 [768, 768], P('mp', 'dp'), may hold values from -0.875 to 0.875
- b_proj: float32 [768], P('dp'), may hold values from -3 to 3
- ffn_gain: float32 [768], P('dp'), may hold values from 0.1 to 1.9
- ffn_shift: float32 [768], P('dp'), may hold values from -1.75 to 1.75
- w_up: float32 [768, 3072], P('dp', 'mp'), may hold values from -0.21875 to 0.21875
- b_up: float32 [3072], P('mp'), may hold values from -3 to 3
- w_down: float32 [3072, 768], P('mp', 'dp'), may hold values from -0.109375 to 0.109375
- b_down: float32 [768], P('dp'), may hold values from -3 to 3
Outputs:
- block_out: bfloat16 [128, 280, 768], P('dp')
- tokens_grad: bfloat16 [128, 280, 768], P('dp')
- attn_gain_grad: float32 [768], P('dp')
- attn_shift_grad: float32 [768], P('dp')
- w_qkv_grad: float32 [768, 3, 768], P('dp', None, 'mp')
- b_qv_grad: float32 [2, 768], P(None, 'mp')
- w_proj_grad: float32 [768, 768], P('mp', 'dp')
- b_proj_grad: float32 [768], P('dp')
- ffn_gain_grad: float32 [768], P('dp')
- ffn_shift_grad: float32 [768], P('dp')
- w_up_grad: float32 [768, 3072], P('dp', 'mp')
- b_up_grad: float32 [3072], P('mp')
- w_down_grad: float32 [3072, 768], P('mp', 'dp')
- b_down_grad: float32 [768], P('dp')
Inputs may be any that keep to these rules, and one draw needn't show every extreme that they name: `patch_counts`: patch count of each pair; in every draw some pair has exactly 240 patches and some exactly 100.
All inputs are finite; a program needn't handle non-finite values.
Results may differ from a plain program's by a relative error of at most 0.022.
Values may be sent and summed in bfloat16 or wider, within the bound.
A program may use at most 192 MiB of HBM per device.

v0:
```python
import math
import jax
import jax.numpy as jnp
from jax import lax
from jax.sharding import PartitionSpec as P

HEADS = 12
HEAD_DIM = 64
TEXT = 40


def normalize(values, gain, shift):
    center = values - jnp.mean(values, axis=-1, keepdims=True)
    spread = jnp.mean(center * center, axis=-1, keepdims=True)
    return center * lax.rsqrt(spread + 1e-06) * gain + shift


def norm_back(values, gain, incoming):
    _, pullback = jax.vjp(lambda member, scaling: normalize(member, scaling, 0.0), values, gain)
    d_values, d_gain = pullback(incoming)
    return (d_values, d_gain, jnp.sum(incoming, axis=(0, 1)))


def per_device(
    patch_counts,
    tokens,
    cotangent,
    attn_gain,
    attn_shift,
    w_qkv,
    b_qv,
    w_proj,
    b_proj,
    ffn_gain,
    ffn_shift,
    w_up,
    b_up,
    w_down,
    b_down,
):
    low_type = jnp.bfloat16
    pair_count, rows_pair, _ = tokens.shape
    head_count = HEADS // lax.axis_size("mp")
    local_width = w_qkv.shape[2]
    score_scale = HEAD_DIM ** (-0.5)
    pair_block = math.gcd(pair_count, -(-512 // rows_pair))
    block_count = pair_count // pair_block
    gathered = (
        lax.all_gather(w_qkv.astype(low_type), "dp", axis=0, tiled=True),
        lax.all_gather(w_proj.astype(low_type), "dp", axis=1, tiled=True),
        lax.all_gather(w_up.astype(low_type), "dp", axis=0, tiled=True),
        lax.all_gather(w_down.astype(low_type), "dp", axis=1, tiled=True),
        lax.all_gather(attn_gain.astype(low_type), "dp", axis=0, tiled=True),
        lax.all_gather(attn_shift.astype(low_type), "dp", axis=0, tiled=True),
        lax.all_gather(b_proj.astype(low_type), "dp", axis=0, tiled=True),
        lax.all_gather(ffn_gain.astype(low_type), "dp", axis=0, tiled=True),
        lax.all_gather(ffn_shift.astype(low_type), "dp", axis=0, tiled=True),
        lax.all_gather(b_down.astype(low_type), "dp", axis=0, tiled=True),
    )
    qkv_full, proj_full, up_full, down_full = (gathered[0], gathered[1], gathered[2], gathered[3])
    gain_one = gathered[4].astype(jnp.float32)
    shift_one = gathered[5].astype(jnp.float32)
    proj_bias = gathered[6].astype(jnp.float32)
    gain_two = gathered[7].astype(jnp.float32)
    shift_two = gathered[8].astype(jnp.float32)
    down_bias = gathered[9].astype(jnp.float32)
    bias_qv = b_qv.astype(low_type).astype(jnp.float32)
    up_bias = b_up.astype(low_type).astype(jnp.float32)
    row_valid = (
        jnp.arange(rows_pair, dtype=jnp.int32)[None, :] < (TEXT + patch_counts)[:, None]
    ).astype(jnp.float32)
    inputs = tokens.astype(jnp.float32)
    normed_one = normalize(inputs, gain_one, shift_one).astype(low_type)
    qkv = jnp.einsum("psd,dtc->pstc", normed_one, qkv_full, preferred_element_type=jnp.float32)
    queries = (qkv[:, :, 0] + bias_qv[0]).astype(low_type)
    key_rows = qkv[:, :, 1].astype(low_type)
    values = (qkv[:, :, 2] + bias_qv[1]).astype(low_type)

    def by_blocks(array):
        return array.reshape(block_count, pair_block, rows_pair, head_count, HEAD_DIM)

    key_mask = row_valid.reshape(block_count, pair_block, rows_pair)

    def score_rows(query_block, key_block, mask_block):
        raw = (
            jnp.einsum(
                "bqhe,bkhe->bhqk", query_block, key_block, preferred_element_type=jnp.float32
            )
            * score_scale
        )
        return jnp.where(mask_block[:, None, None, :] > 0, raw, -1e30)

    def attend(operands):
        query_block, key_block, value_block, mask_block = operands
        scores = score_rows(query_block, key_block, mask_block)
        row_max = jnp.max(scores, axis=-1, keepdims=True)
        expo = jnp.exp(scores - row_max)
        row_total = jnp.sum(expo, axis=-1, keepdims=True)
        probabilities = (expo / row_total).astype(low_type)
        attended_block = jnp.einsum(
            "bhqk,bkhe->bqhe", probabilities, value_block, preferred_element_type=jnp.float32
        ).astype(low_type)
        log_total = row_max[..., 0] + jnp.log(row_total[..., 0])
        return (attended_block, log_total)

    attended_blocks, log_totals = lax.map(
        attend, (by_blocks(queries), by_blocks(key_rows), by_blocks(values), key_mask)
    )
    attended = attended_blocks.reshape(pair_count, rows_pair, local_width)
    proj_part = jnp.einsum("psc,cd->psd", attended, proj_full, preferred_element_type=jnp.float32)
    attn_sum = lax.psum(proj_part.astype(jnp.bfloat16), "mp").astype(jnp.float32)
    hidden = inputs + attn_sum + proj_bias
    normed_two = normalize(hidden, gain_two, shift_two).astype(low_type)
    pre_act = (
        jnp.einsum("psd,df->psf", normed_two, up_full, preferred_element_type=jnp.float32) + up_bias
    )
    active = jax.nn.gelu(pre_act, approximate=False).astype(low_type)
    down_part = jnp.einsum("psf,fd->psd", active, down_full, preferred_element_type=jnp.float32)
    mlp_sum = lax.psum(down_part.astype(jnp.bfloat16), "mp").astype(jnp.float32)
    block_out = ((hidden + mlp_sum + down_bias) * row_valid[:, :, None]).astype(low_type)
    qkv_back, proj_back, up_back, down_back = (qkv_full, proj_full, up_full, down_full)
    gain_one_back, gain_two_back = (gain_one, gain_two)
    upstream = cotangent.astype(jnp.float32) * row_valid[:, :, None]
    upstream_low = upstream.astype(low_type)
    grad_b_down = jnp.sum(upstream, axis=(0, 1))
    grad_w_down = jnp.einsum(
        "psf,psd->fd", active, upstream_low, preferred_element_type=jnp.float32
    )
    d_active = jnp.einsum(
        "psd,fd->psf", upstream_low, down_back, preferred_element_type=jnp.float32
    )
    _, gelu_pull = jax.vjp(lambda member: jax.nn.gelu(member, approximate=False), pre_act)
    d_pre = gelu_pull(d_active)[0].astype(low_type)
    grad_b_up = jnp.sum(d_pre, axis=(0, 1), dtype=jnp.float32)
    grad_w_up = jnp.einsum("psd,psf->df", normed_two, d_pre, preferred_element_type=jnp.float32)
    d_normed_two = lax.psum(
        jnp.einsum("psf,df->psd", d_pre, up_back, preferred_element_type=jnp.float32).astype(
            jnp.bfloat16
        ),
        "mp",
    ).astype(jnp.float32)
    d_hidden_norm, grad_gain_two, grad_shift_two = norm_back(hidden, gain_two_back, d_normed_two)
    d_hidden = upstream + d_hidden_norm
    grad_b_proj = jnp.sum(d_hidden, axis=(0, 1))
    d_hidden_low = d_hidden.astype(low_type)
    grad_w_proj = jnp.einsum(
        "psc,psd->cd", attended, d_hidden_low, preferred_element_type=jnp.float32
    )
    d_attended = jnp.einsum(
        "psd,cd->psc", d_hidden_low, proj_back, preferred_element_type=jnp.float32
    ).astype(low_type)

    def attend_back(operands):
        query_block, key_block, value_block, mask_block, log_total, d_out = operands
        scores = score_rows(query_block, key_block, mask_block)
        probabilities = jnp.exp(scores - log_total[..., None])
        d_probs = jnp.einsum(
            "bqhe,bkhe->bhqk", d_out, value_block, preferred_element_type=jnp.float32
        )
        d_value = jnp.einsum(
            "bhqk,bqhe->bkhe",
            probabilities.astype(low_type),
            d_out,
            preferred_element_type=jnp.float32,
        )
        inner = jnp.sum(probabilities * d_probs, axis=-1, keepdims=True)
        d_scores = (probabilities * (d_probs - inner)).astype(low_type)
        d_query = score_scale * jnp.einsum(
            "bhqk,bkhe->bqhe", d_scores, key_block, preferred_element_type=jnp.float32
        )
        d_key = score_scale * jnp.einsum(
            "bhqk,bqhe->bkhe", d_scores, query_block, preferred_element_type=jnp.float32
        )
        return jnp.stack([d_query, d_key, d_value], axis=2).astype(low_type)

    d_blocks = lax.map(
        attend_back,
        (
            by_blocks(queries),
            by_blocks(key_rows),
            by_blocks(values),
            key_mask,
            log_totals,
            by_blocks(d_attended),
        ),
    )
    d_qkv = d_blocks.reshape(pair_count, rows_pair, 3, local_width)
    column_sums = jnp.sum(d_qkv, axis=(0, 1), dtype=jnp.float32)
    grad_b_qv = jnp.stack([column_sums[0], column_sums[2]], axis=0)
    grad_w_qkv = jnp.einsum("psd,pstc->dtc", normed_one, d_qkv, preferred_element_type=jnp.float32)
    d_normed_one = lax.psum(
        jnp.einsum("pstc,dtc->psd", d_qkv, qkv_back, preferred_element_type=jnp.float32).astype(
            jnp.bfloat16
        ),
        "mp",
    ).astype(jnp.float32)
    d_input_norm, grad_gain_one, grad_shift_one = norm_back(inputs, gain_one_back, d_normed_one)
    tokens_grad = (d_hidden + d_input_norm).astype(low_type)
    bias_grads = lax.psum((grad_b_qv, grad_b_up), "dp")
    summed = (
        lax.psum_scatter(grad_w_qkv, "dp", scatter_dimension=0, tiled=True),
        lax.psum_scatter(grad_w_proj, "dp", scatter_dimension=1, tiled=True),
        lax.psum_scatter(grad_w_up, "dp", scatter_dimension=0, tiled=True),
        lax.psum_scatter(grad_w_down, "dp", scatter_dimension=1, tiled=True),
        lax.psum_scatter(grad_gain_one, "dp", scatter_dimension=0, tiled=True),
        lax.psum_scatter(grad_shift_one, "dp", scatter_dimension=0, tiled=True),
        lax.psum_scatter(grad_b_proj, "dp", scatter_dimension=0, tiled=True),
        lax.psum_scatter(grad_gain_two, "dp", scatter_dimension=0, tiled=True),
        lax.psum_scatter(grad_shift_two, "dp", scatter_dimension=0, tiled=True),
        lax.psum_scatter(grad_b_down, "dp", scatter_dimension=0, tiled=True),
    )
    out_qkv, out_proj, out_up, out_down = (summed[0], summed[1], summed[2], summed[3])
    out_gain_one, out_shift_one, out_bproj = (summed[4], summed[5], summed[6])
    out_gain_two, out_shift_two, out_bdown = (summed[7], summed[8], summed[9])
    return (
        block_out,
        tokens_grad,
        out_gain_one,
        out_shift_one,
        out_qkv,
        bias_grads[0],
        out_proj,
        out_bproj,
        out_gain_two,
        out_shift_two,
        out_up,
        bias_grads[1],
        out_down,
        out_bdown,
    )


def solution(mesh):
    in_specs = (
        P("dp"),
        P("dp", None, None),
        P("dp", None, None),
        P("dp"),
        P("dp"),
        P("dp", None, "mp"),
        P(None, "mp"),
        P("mp", "dp"),
        P("dp"),
        P("dp"),
        P("dp"),
        P("dp", "mp"),
        P("mp"),
        P("mp", "dp"),
        P("dp"),
    )
    out_specs = (
        P("dp", None, None),
        P("dp", None, None),
        P("dp"),
        P("dp"),
        P("dp", None, "mp"),
        P(None, "mp"),
        P("mp", "dp"),
        P("dp"),
        P("dp"),
        P("dp"),
        P("dp", "mp"),
        P("mp"),
        P("mp", "dp"),
        P("dp"),
    )
    return jax.shard_map(
        per_device, mesh=mesh, in_specs=in_specs, out_specs=out_specs, check_vma=False
    )
```

profile of v0, /device:TPU:0, one launch (start us, length us, event | category | flops | bytes accessed | tf_op | source)
XLA Modules:
  0.0 1070.2 jit_solution(13060933296893398383)
XLA Ops:
  20.8 63.2 %all-reduce.13 = (bf16[768]{0:T(1024)(128)(2,1)}, bf16[768]{0:T(1024)(128)(2,1)}, bf16[768]{0:T(1024)(128)(2,1)}, bf16[768]{0:T(1024)(128)(2,1)}, bf16[768]{0:T(1024)(128)(2,1)}, /*index=5*/bf16[768]{0:T(1024)(128)(2,1)}) all-reduce(bf16[768]{0:T(1024)(128)(2,1)} %dynamic-update-slice.4, ...), channel_id=1, replica_groups=mesh['dp'=16,'mp'=2] {'dp'}, use_global_device_ids=true, to_apply=%add.4 | all-reduce | flops 4608 | bytes 18432
  90.3 2.5 convert_reduce_fusion.4
  92.9 3.1 fusion.74
  97.2 20.3 %all_gather.33 = bf16[384,768]{0,1:T(8,128)(2,1)} all-gather(bf16[384,48]{0,1:T(8,128)(2,1)S(1)} %convert_element_type.183), channel_id=1, replica_groups=mesh['dp'=16,'mp'=2] {'dp'}, dimensions={1}, use_global_device_ids=true | all-gather | bytes 626688 | tf_op jit(solution)/shard_map/all_gather | solution.py:50
  117.5 7.1 fusion.96
  124.6 3.3 fusion.113
  129.4 6.0 copy.58
  135.3 5.5 copy.59
  140.8 4.0 copy.60
  144.8 7.3 add_convert_fusion.3
  152.2 32.6 %while.22 = (s32[]{:T(128)}, bf16[4,2,280,6,64]{2,4,3,1,0:T(8,128)(2,1)}, f32[4,2,6,280]{3,2,1,0:T(8,128)S(1)}, bf16[4,2,280,6,64]{2,4,3,1,0:T(8,128)(2,1)}, f32...) while((s32[]{:T(128)}, ...), condition=%wide.region_5.6_spmd, body=%wide.region_2.5_spmd.sunk | while | flops 252346640 | bytes 13796445 | solution.py:106
  152.9 2.7 fusion.143
  156.9 3.5 fusion.145
  161.0 2.7 fusion.143
  165.0 3.5 fusion.145
  169.2 2.7 fusion.143
  173.2 3.5 fusion.145
  177.3 2.7 fusion.143
  181.3 3.5 fusion.145
  184.8 6.0 convolution_convert_fusion.2
  198.1 83.8 %all-reduce.19.cloned.1.call-done = bf16[8,280,768]{2,1,0:T(8,128)(2,1)} async-done(((bf16[8,280,768]{2,1,0:T(8,128)(2,1)}), bf16[8,280,768]{2,1,0:T(8,128)(2,1)}) %all-reduce.19.cloned.1.call-update) | async-done | bytes 3440656 | tf_op jit(solution)/shard_map/psum | solution.py:111
  281.9 3.3 fusion.82
  288.5 38.6 %all-gather.6.cloned.1.call-done = bf16[768,1536]{1,0:T(8,128)(2,1)} async-done(((bf16[48,1536]{1,0:T(8,128)(2,1)}), bf16[768,1536]{1,0:T(8,128)(2,1)}) %all-gather.6.cloned.1.call-update) | async-done | bytes 2359312 | tf_op jit(solution)/shard_map/all_gather | solution.py:51
  327.1 13.9 %fusion.86 = (u8[280,1536]{1,0:T(8,128)(4,1)S(1)}, u8[280,1536]{1,0:T(8,128)(4,1)S(1)}, f32[8,280,1536]{2,1,0:T(8,128)S(1)}) fusion(f32[1536]{0:T(1024)} %convert_convert_fusion, bf16[768,1536]{1,0:T(8,128)(2,1)} %all-gather.6.cloned.1.call-done, f32[768]{0:T(1024)} %convert_element_type.191, f32[768]{0:T(1024)} %convert_element_type.189, ...), kind=kOutput, calls=%fused_computation.134 | convolution fusion | flops 5347614720 | bytes 23896576 | tf_op jit(solution)/shard_map/psd,df->psf/dot_general | solution.py:115
  341.0 4.9 copy-done.6
  346.0 32.9 %multiply_convert_fusion.1 = (bf16[8,280,1536]{2,1,0:T(8,128)(2,1)}, f32[8,280,1536]{2,1,0:T(8,128)}) fusion(f32[8,280,1536]{2,1,0:T(8,128)S(1)} %get-tuple-element.187, f32[1536]{0:T(1024)S(1)} %copy-done.25, u8[280,1536]{1,0:T(8,128)(4,1)S(1)} %get-tuple-element.113, u8[280,1536]{1,0:T(8,128)(4,1)S(1)} %get-tuple-element.112), kind=kLoop, calls=%fused_computation.75 | loop fusion | flops 244285440 | bytes 35272704 | tf_op jit(solution)/shard_map/convert_element_type | solution.py:117
  378.9 18.8 %convert_reduce_fusion.1 = (f32[1536]{0:T(1024)}, bf16[8,280,1536]{2,1,0:T(8,128)(2,1)}) fusion(f32[8,280,1536]{2,1,0:T(8,128)} %get-tuple-element.173, bf16[1536,768]{0,1:T(8,128)(2,1)} %all-gather.8.cloned.1.call-done, bf16[8,280,768]{2,1,0:T(8,128)(2,1)} %param.21, f32[8,280]{1,0:T(8,128)} %fusion.108, f32[8,280,1536]{2,1,0:T(8,128)} %copy-done.6, ...), kind=kOutput, calls=%fused_computation.73 | convolution fusion | flops 5348473344 | bytes 40227584 | tf_op jit(solution)/shard_map/psd,fd->psf/dot_general | solution.py:129
  397.6 10.0 convolution_convert_fusion
  407.7 10.0 convolution_convert_fusion.1
  417.7 81.1 %all-reduce.21.cloned.1.call-done = bf16[8,280,768]{2,1,0:T(8,128)(2,1)} async-done(((bf16[8,280,768]{2,1,0:T(8,128)(2,1)}), bf16[8,280,768]{2,1,0:T(8,128)(2,1)}) %all-reduce.21.cloned.1.call-update) | async-done | bytes 3440656 | tf_op jit(solution)/shard_map/psum | solution.py:136
  498.8 6.4 convert_reduce_fusion.3
  505.2 5.6 fusion.77
  510.8 4.9 fusion.111
  515.7 2.7 copy-done.3
  518.5 3.2 convolution_convert_fusion.3
  521.6 4.0 copy.62
  525.6 64.1 %while.23 = (s32[]{:T(128)}, bf16[4,2,280,3,6,64]{2,5,4,1,3,0:T(8,128)(2,1)}, bf16[4,2,280,6,64]{2,4,3,1,0:T(8,128)(2,1)}, f32[4,2,280]{2,1,0:T(2,128)}, bf16[4,...) while((s32[]{:T(128)}, ...), condition=%wide.region_15.16_spmd, body=%wide.region_13.15_spmd.sunk | while | flops 621167104 | bytes 36805476 | solution.py:176
  526.0 2.3 fusion.154
  529.1 3.4 multiply_reduce_fusion.3
  538.0 2.5 fusion.155
  545.0 3.4 multiply_reduce_fusion.3
  553.9 2.5 fusion.155
  557.9 2.3 fusion.154
  560.9 3.4 multiply_reduce_fusion.3
  569.8 2.5 fusion.155
  573.7 2.3 fusion.154
  576.8 3.4 multiply_reduce_fusion.3
  585.7 2.5 fusion.155
  589.7 4.3 copy.63
  594.0 2.9 copy-done.7
  596.9 7.7 bitcast_convert_fusion
  604.8 7.4 fusion.101
  612.3 12.6 %convolution_bitcast_fusion.1 = f32[768,1536]{1,0:T(8,128)} fusion(bf16[8,280,1536]{2,1,0:T(8,128)(2,1)} %get-tuple-element.189, f32[768]{0:T(1024)S(1)} %copy-done.35, f32[768]{0:T(1024)S(1)} %copy-done.24, f32[8,280]{1,0:T(8,128)S(1)} %copy-done.20, f32[8,280]{1,0:T(8,128)S(1)} %broadcast_multiply_fusion, f32[768]{0:T(1024)S(1)} %convert_element_type.187, ...), kind=kOutput, calls=%fused_computation.130 | convolution fusion | flops 5300305920 | bytes 18508288 | tf_op jit(solution)/shard_map/psd,psf->df/dot_general | solution.py:135
  625.0 11.0 %convolution_bitcast_fusion = f32[1536,768]{0,1:T(8,128)} fusion(bf16[8,280,1536]{2,1,0:T(8,128)(2,1)} %get-tuple-element.172, bf16[8,280,768]{2,1,0:T(8,128)(2,1)} %param.21, f32[8,280]{1,0:T(8,128)S(1)} %copy-done.18), kind=kOutput, calls=%fused_computation.129 | convolution fusion | flops 5289984000 | bytes 15049472 | tf_op jit(solution)/shard_map/psf,psd->fd/dot_general | solution.py:126
  636.3 13.7 %convolution_bitcast_fusion.2 = f32[768,3,384]{2,0,1:T(8,128)} fusion(bf16[8,280,3,384]{1,3,2,0:T(8,128)(2,1)} %bitcast.170, bf16[8,280,768]{2,1,0:T(8,128)(2,1)S(1)} %copy-done, f32[768]{0:T(1024)S(1)} %copy-done.34, f32[768]{0:T(1024)S(1)} %copy-done.22, f32[8,280]{1,0:T(8,128)S(1)} %copy-done.16, f32[8,280]{1,0:T(8,128)S(1)} %copy-done.11), kind=kOutput, calls=%fused_computation.144 | convolution fusion | flops 3973939200 | bytes 12164608 | tf_op jit(solution)/shard_map/psd,pstc->dtc/dot_general | solution.py:190
  650.7 4.3 convert_reduce_fusion
  655.3 115.5 %all-reduce.23.cloned.1.call-done = (bf16[8,280,768]{2,1,0:T(8,128)(2,1)}, bf16[8,280,768]{2,1,0:T(8,128)(2,1)}) async-done(((bf16[8,280,768]{2,1,0:T(8,128)(2,1)}, bf16[8,280,768]{2,1,0:T(8,128)(2,1)}), (bf16[8,280,768]{2,1,0:T(8,128)(2,1)}, bf16[8,280,768]{2,1,0:T(8,128)(2,1)})) %all-reduce.23.cloned.1.call-update) | async-done | bytes 6881296 | tf_op jit(solution)/shard_map/psum | solution.py:119
  770.7 4.2 convert_reduce_fusion.2
  774.9 4.3 fusion.78
  779.3 61.8 %all-reduce.12 = (f32[768]{0:T(1024)S(1)}, f32[768]{0:T(1024)S(1)}, f32[2,384]{1,0:T(2,128)}, f32[768]{0:T(1024)}, f32[768]{0:T(1024)}, /*index=5*/f32[768]{0:T(1024)}, f32[1536]{0:T(1024)}, f32[768]{0:T(1024)S(1)}) all-reduce(f32[768]{0:T(1024)S(1)} %get-tuple-element.116, ...), channel_id=2, replica_groups=mesh['dp'=16,'mp'=2] {'dp'}, use_global_device_ids=true, to_apply=%region_20.21.clone | all-reduce | flops 6912 | bytes 55296
  846.6 11.0 %add_convert_fusion.1 = (bf16[8,280,768]{2,1,0:T(8,128)(2,1)}, bf16[8,280,768]{2,1,0:T(8,128)(2,1)}) fusion(f32[8,280,768]{2,1,0:T(8,128)} %copy-done.3, bf16[8,280,768]{2,1,0:T(8,128)(2,1)S(1)} %copy-done, bf16[8,280,768]{2,1,0:T(8,128)(2,1)} %get-tuple-element.169, f32[8,280]{1,0:T(8,128)S(1)} %negate_multiply_fusion.1, ...), kind=kLoop, calls=%fused_computation.116 | loop fusion | flops 32686080 | bytes 27579136 | tf_op jit(solution)/shard_map/convert_element_type | solution.py:198
  857.6 54.7 %reduce-scatter.9.cloned.1.call-done = f32[48,1536]{1,0:T(8,128)} async-done(((f32[768,1536]{1,0:T(8,128)}), f32[48,1536]{1,0:T(8,128)}) %reduce-scatter.9.cloned.1.call-update) | async-done | bytes 294928 | tf_op jit(solution)/shard_map/reduce_scatter | solution.py:203
  912.3 79.2 %reduce-scatter.11.cloned.1.call-done = f32[1536,48]{0,1:T(8,128)} async-done(((f32[1536,768]{0,1:T(8,128)}), f32[1536,48]{0,1:T(8,128)}) %reduce-scatter.11.cloned.1.call-update) | async-done | bytes 294928 | tf_op jit(solution)/shard_map/reduce_scatter | solution.py:204
  991.5 71.6 %reduce-scatter.5.cloned.1.call-done = f32[48,3,384]{2,0,1:T(8,128)} async-done(((f32[768,3,384]{2,0,1:T(8,128)}), f32[48,3,384]{2,0,1:T(8,128)}) %reduce-scatter.5.cloned.1.call-update) | async-done | bytes 221200 | tf_op jit(solution)/shard_map/reduce_scatter | solution.py:201
  (202 shorter events, 79.9 us)
Async XLA Ops:
  7.2 110.4 %copy-start = (bf16[8,280,768]{2,1,0:T(8,128)(2,1)S(1)}, bf16[8,280,768]{2,1,0:T(8,128)(2,1)}, u32[]{:S(2)}) copy-start(bf16[8,280,768]{2,1,0:T(8,128)(2,1)} %param.20) | copy-start | bytes 10321924
  7.2 110.3 %all-gather.4.cloned.1.call-start = ((), (), s32[]{:S(2)}) async-start(), calls=%async_computation.4 | async-start | bytes 1880064 | tf_op jit(solution)/shard_map/all_gather | solution.py:49
  9.0 272.9 %all-reduce.19.cloned.1.call-start = ((), (), s32[]{:S(2)}) async-start(), calls=%async_computation.5 | async-start | bytes 6881280 | tf_op jit(solution)/shard_map/psum | solution.py:111
  18.0 0.6 copy-start.33
  84.7 39.9 %copy-start.21 = (f32[768]{0:T(1024)}, f32[768]{0:T(1024)S(1)}, u32[]{:S(2)}) copy-start(f32[768]{0:T(1024)S(1)} %convert_element_type.172) | copy-start | bytes 9220
  88.7 1.6 copy-start.38
  92.9 31.7 %copy-start.10 = (f32[8,280]{1,0:T(8,128)}, f32[8,280]{1,0:T(8,128)S(1)}, u32[]{:S(2)}) copy-start(f32[8,280]{1,0:T(8,128)S(1)} %broadcast_multiply_fusion.1) | copy-start | bytes 26884
  96.0 0.6 copy-start.12
  135.3 9.5 copy-start.28
  135.3 9.5 copy-start.29
  184.8 9.5 copy-start.39
  184.8 12.1 %copy-start.37 = (bf16[768]{0:T(1024)(128)(2,1)S(1)}, bf16[768]{0:T(1024)(128)(2,1)}, u32[]{:S(2)}) copy-start(bf16[768]{0:T(1024)(128)(2,1)} %get-tuple-element.162) | copy-start | bytes 4612
  184.8 12.7 %copy-start.32 = (f32[1536]{0:T(1024)S(1)}, f32[1536]{0:T(1024)}, u32[]{:S(2)}) copy-start(f32[1536]{0:T(1024)} %param.31) | copy-start | bytes 18436
  190.8 136.3 %all-gather.6.cloned.1.call-start = ((), (), s32[]{:S(2)}) async-start(), calls=%async_computation.6 | async-start | bytes 2506752 | tf_op jit(solution)/shard_map/all_gather | solution.py:51
  192.5 186.3 %all-gather.8.cloned.1.call-start = ((), (), s32[]{:S(2)}) async-start(), calls=%async_computation.7 | async-start | bytes 2506752 | tf_op jit(solution)/shard_map/all_gather | solution.py:52
  194.2 304.6 %all-reduce.21.cloned.1.call-start = ((), (), s32[]{:S(2)}) async-start(), calls=%async_computation.8 | async-start | bytes 6881280 | tf_op jit(solution)/shard_map/psum | solution.py:136
  281.9 3.3 copy-start.1
  287.3 0.6 copy-start.14
  327.1 18.9 %copy-start.25 = (f32[1536]{0:T(1024)S(1)}, f32[1536]{0:T(1024)}, u32[]{:S(2)}) copy-start(f32[1536]{0:T(1024)} %convert_convert_fusion) | copy-start | bytes 18436
  341.0 5.0 copy-start.6
  378.9 18.8 %copy-start.40 = (bf16[768,1536]{1,0:T(8,128)(2,1)S(1)}, bf16[768,1536]{1,0:T(8,128)(2,1)}, u32[]{:S(2)}) copy-start(bf16[768,1536]{1,0:T(8,128)(2,1)} %all-gather.6.cloned.1.call-done) | copy-start | bytes 7077892
  407.7 363.0 %all-reduce.23.cloned.1.call-start = ((), (), s32[]{:S(2)}) async-start(), calls=%async_computation.13 | async-start | bytes 13762560 | tf_op jit(solution)/shard_map/psum | solution.py:119
  498.8 6.4 copy-start.15
  498.8 6.4 copy-start.2
  498.8 6.4 copy-start.5
  498.8 6.4 copy-start.19
  498.8 6.4 copy-start.23
  505.2 5.6 copy-start.8
  505.2 5.6 copy-start.17
  510.8 7.6 copy-start.9
  515.7 2.8 copy-start.3
  589.7 7.2 copy-start.41
  594.0 2.9 copy-start.7
  604.6 7.7 copy-start.20
  604.6 7.7 copy-start.24
  604.6 7.7 copy-start.35
  604.6 253.0 %reduce-scatter.7.cloned.1.call-start = ((), (), s32[]{:S(2)}) async-start(), calls=%async_computation.10 | async-start | bytes 1253376 | tf_op jit(solution)/shard_map/reduce_scatter | solution.py:202
  612.2 12.8 %copy-start.18 = (f32[8,280]{1,0:T(8,128)S(1)}, f32[8,280]{1,0:T(8,128)}, u32[]{:S(2)}) copy-start(f32[8,280]{1,0:T(8,128)} %fusion.108) | copy-start | bytes 26884
  612.2 300.1 %reduce-scatter.9.cloned.1.call-start = ((), (), s32[]{:S(2)}) async-start(), calls=%async_computation.11 | async-start | bytes 5013504 | tf_op jit(solution)/shard_map/reduce_scatter | solution.py:203
  624.9 11.4 %copy-start.11 = (f32[8,280]{1,0:T(8,128)S(1)}, f32[8,280]{1,0:T(8,128)}, u32[]{:S(2)}) copy-start(f32[8,280]{1,0:T(8,128)} %copy-done.10) | copy-start | bytes 26884
  624.9 11.4 %copy-start.16 = (f32[8,280]{1,0:T(8,128)S(1)}, f32[8,280]{1,0:T(8,128)}, u32[]{:S(2)}) copy-start(f32[8,280]{1,0:T(8,128)} %fusion.109) | copy-start | bytes 26884
  624.9 11.4 %copy-start.22 = (f32[768]{0:T(1024)S(1)}, f32[768]{0:T(1024)}, u32[]{:S(2)}) copy-start(f32[768]{0:T(1024)} %copy-done.21) | copy-start | bytes 9220
  624.9 11.4 %copy-start.34 = (f32[768]{0:T(1024)S(1)}, f32[768]{0:T(1024)}, u32[]{:S(2)}) copy-start(f32[768]{0:T(1024)} %convert_element_type.174) | copy-start | bytes 9220
  624.9 366.6 %reduce-scatter.11.cloned.1.call-start = ((), (), s32[]{:S(2)}) async-start(), calls=%async_computation.12 | async-start | bytes 5013504 | tf_op jit(solution)/shard_map/reduce_scatter | solution.py:204
  636.0 14.1 %copy-start.36 = (bf16[768]{0:T(1024)(128)(2,1)S(1)}, bf16[768]{0:T(1024)(128)(2,1)}, u32[]{:S(2)}) copy-start(bf16[768]{0:T(1024)(128)(2,1)} %get-tuple-element.167) | copy-start | bytes 4612
  636.0 427.1 %reduce-scatter.5.cloned.1.call-start = ((), (), s32[]{:S(2)}) async-start(), calls=%async_computation.9 | async-start | bytes 3760128 | tf_op jit(solution)/shard_map/reduce_scatter | solution.py:201
  650.7 124.2 %copy-start.13 = (f32[8,280]{1,0:T(8,128)S(1)}, f32[8,280]{1,0:T(8,128)}, u32[]{:S(2)}) copy-start(f32[8,280]{1,0:T(8,128)} %copy-done.12) | copy-start | bytes 26884
  770.7 4.2 copy-start.4
  770.7 8.5 copy-start.26
  770.7 8.5 copy-start.27
  770.7 8.5 copy-start.30
  770.7 8.5 copy-start.31
Sparse Core Ops, SparseCore 0:
  10.9 43.1 all-gather.3
  190.9 90.9 all-reduce.18
  284.8 42.3 all-gather.5
  329.8 41.0 all-gather.7
  407.8 90.9 all-reduce.20
  604.7 165.9 all-reduce.22
  774.9 58.1 reduce-scatter.6
  837.6 74.6 reduce-scatter.8
  916.7 74.7 reduce-scatter.10
  995.8 67.3 reduce-scatter.4
where the time goes:
time: 1080 us; the launch traced here: 1070 us
  waiting for transfers between devices  525 us (49%)
  matrix products  194 us (18%)
  blocking collectives  145 us (13%)
  other arithmetic  136 us (13%)
  local copies, waits for them, and re-layouts  53.1 us (5%)
  between operations  16.2 us (2%)
    unnamed x2, blocking collectives  125 us
    psum x1, waiting for transfers between devices, per_device(): mlp_sum = lax.psum(down_part.astype(jnp.bfloat16), 'mp').astype(jnp.float32)  115 us
    psum x1, waiting for transfers between devices, per_device(): lax.psum(proj_part.astype(jnp.bfloat16), 'mp').astype(jnp.float32)  83.8 us
    psum x1, waiting for transfers between devices, per_device(): lax.psum(jnp.einsum('psf,df->psd', d_pre, up_back, preferred_element_type...  81.1 us
    reduce_scatter x1, waiting for transfers between devices, per_device(): lax.psum_scatter(grad_w_down, 'dp', scatter_dimension=1, tiled=True)  79.2 us
    reduce_scatter x1, waiting for transfers between devices, per_device(): lax.psum_scatter(grad_w_qkv, 'dp', scatter_dimension=0, tiled=True)  71.6 us
    reduce_scatter x1, waiting for transfers between devices, per_device(): lax.psum_scatter(grad_w_up, 'dp', scatter_dimension=0, tiled=True)  54.7 us
    all_gather x1, waiting for transfers between devices, per_device(): lax.all_gather(w_up.astype(low_type), 'dp', axis=0, tiled=True)  38.6 us
  transfers between devices with their start and end apart: 10, of which 7 were waited for; matrix products, arithmetic and copies ran while one was open for 16% of the time, Pallas kernels for 0%

commit v1 on v0

--- a/solution.py
+++ b/solution.py
@@ -38,6 +38,20 @@
     w_down,
     b_down,
 ):
+
+    def treat_notes(mine_x):
+        step_out, taken_in = (lax.axis_size("dp"), lax.axis_index("dp"))
+        back, mixed_arr = (mine_x, 1)
+        while mixed_arr < step_out:
+            out_arr = lax.ppermute(
+                back, axis_name="dp", perm=tuple(((s, s ^ mixed_arr) for s in range(step_out)))
+            )
+            arr_out = jnp.concatenate([back, out_arr], 0)
+            all_rows = jnp.concatenate([out_arr, back], 0)
+            back = jnp.where(taken_in & mixed_arr == 0, arr_out, all_rows)
+            mixed_arr = 2 * mixed_arr
+        return back
+
     low_type = jnp.bfloat16
     pair_count, rows_pair, _ = tokens.shape
     head_count = HEADS // lax.axis_size("mp")
@@ -48,7 +62,7 @@
     gathered = (
         lax.all_gather(w_qkv.astype(low_type), "dp", axis=0, tiled=True),
         lax.all_gather(w_proj.astype(low_type), "dp", axis=1, tiled=True),
-        lax.all_gather(w_up.astype(low_type), "dp", axis=0, tiled=True),
+        treat_notes(w_up.astype(low_type)),
         lax.all_gather(w_down.astype(low_type), "dp", axis=1, tiled=True),
         lax.all_gather(attn_gain.astype(low_type), "dp", axis=0, tiled=True),
         lax.all_gather(attn_shift.astype(low_type), "dp", axis=0, tiled=True),

time: 1080 us -> 1040 us (0.963)
  waiting for transfers between devices: 525 us -> 477 us
    all_gather x1 -> x0, waiting for transfers between devices: 38.6 us -> none  [per_device(): lax.all_gather(w_up.astype(low_type), 'dp', axis=0, tiled=True)]
    psum x1, waiting for transfers between devices: 83.8 us -> 55.2 us  [per_device(): lax.psum(proj_part.astype(jnp.bfloat16), 'mp').astype(jnp.float32)]
    ppermute x0 -> x4, waiting for transfers between devices: none -> 18.3 us  [treat_notes(): lax.ppermute(back, axis_name='dp', perm=tuple(((s, s ^ mixed_arr) for s i...]
    unnamed x103 -> x99, local copies, waits for them, and re-layouts: 23.1 us -> 18.1 us
  transfers between devices with their start and end apart: 10 -> 13, of which waited for: 7 -> 9; matrix products, arithmetic and copies ran while one was open for 16% -> 18% of each run, Pallas kernels for 0% -> 0%
where the time goes in v1:
time: 1040 us; the launch traced here: 1030 us
  waiting for transfers between devices  477 us (46%)
  matrix products  199 us (19%)
  other arithmetic  145 us (14%)
  blocking collectives  145 us (14%)
  local copies, waits for them, and re-layouts  47.8 us (5%)
  between operations  15.9 us (2%)
    unnamed x2, blocking collectives  125 us
    psum x1, waiting for transfers between devices, per_device(): mlp_sum = lax.psum(down_part.astype(jnp.bfloat16), 'mp').astype(jnp.float32)  115 us
    psum x1, waiting for transfers between devices, per_device(): lax.psum(jnp.einsum('psf,df->psd', d_pre, up_back, preferred_element_type...  82.5 us
    reduce_scatter x1, waiting for transfers between devices, per_device(): lax.psum_scatter(grad_w_down, 'dp', scatter_dimension=1, tiled=True)  79.2 us
    reduce_scatter x1, waiting for transfers between devices, per_device(): lax.psum_scatter(grad_w_qkv, 'dp', scatter_dimension=0, tiled=True)  71.9 us
    psum x1, waiting for transfers between devices, per_device(): lax.psum(proj_part.astype(jnp.bfloat16), 'mp').astype(jnp.float32)  55.2 us
    reduce_scatter x1, waiting for transfers between devices, per_device(): lax.psum_scatter(grad_w_up, 'dp', scatter_dimension=0, tiled=True)  54.5 us
    convert_element_type x1, other arithmetic, per_device(): active = jax.nn.gelu(pre_act, approximate=False).astype(low_type)  34.4 us
  transfers between devices with their start and end apart: 13, of which 9 were waited for; matrix products, arithmetic and copies ran while one was open for 18% of the time, Pallas kernels for 0%

profile of v1, /device:TPU:0, one launch (start us, length us, event | category | flops | bytes accessed | tf_op | source)
XLA Modules:
  0.0 1033.5 jit_solution(330288182911182065)
XLA Ops:
  20.8 63.2 %all-reduce.13 = (bf16[768]{0:T(1024)(128)(2,1)}, bf16[768]{0:T(1024)(128)(2,1)}, bf16[768]{0:T(1024)(128)(2,1)}, bf16[768]{0:T(1024)(128)(2,1)}, bf16[768]{0:T(1024)(128)(2,1)}, /*index=5*/bf16[768]{0:T(1024)(128)(2,1)}) all-reduce(bf16[768]{0:T(1024)(128)(2,1)} %dynamic-update-slice.4, ...), channel_id=1, replica_groups=mesh['dp'=16,'mp'=2] {'dp'}, use_global_device_ids=true, to_apply=%add.4 | all-reduce | flops 4608 | bytes 18432
  90.3 2.5 convert_reduce_fusion.4
  92.9 3.1 fusion.74
  97.2 20.3 %all_gather.30 = bf16[384,768]{0,1:T(8,128)(2,1)} all-gather(bf16[384,48]{0,1:T(8,128)(2,1)S(1)} %convert_element_type.183), channel_id=1, replica_groups=mesh['dp'=16,'mp'=2] {'dp'}, dimensions={1}, use_global_device_ids=true | all-gather | bytes 626688 | tf_op jit(solution)/shard_map/all_gather | solution.py:64
  117.5 7.1 fusion.94
  124.6 3.3 fusion.116
  129.3 5.7 copy.58
  135.0 5.5 copy.59
  140.5 4.0 copy.60
  144.5 7.3 add_convert_fusion.3
  151.8 32.6 %while.22 = (s32[]{:T(128)}, bf16[4,2,280,6,64]{2,4,3,1,0:T(8,128)(2,1)}, f32[4,2,6,280]{3,2,1,0:T(8,128)S(1)}, bf16[4,2,280,6,64]{2,4,3,1,0:T(8,128)(2,1)}, f32...) while((s32[]{:T(128)}, ...), condition=%wide.region_5.6_spmd, body=%wide.region_2.5_spmd.sunk | while | flops 252346640 | bytes 13796445 | solution.py:120
  152.5 2.7 fusion.146
  156.5 3.5 fusion.148
  160.7 2.7 fusion.146
  164.7 3.5 fusion.148
  168.9 2.7 fusion.146
  172.9 3.5 fusion.148
  177.0 2.7 fusion.146
  181.0 3.5 fusion.148
  184.5 6.0 convolution_convert_fusion.2
  198.0 7.8 collective-permute-done.1
  214.3 9.1 collective-permute-done.2
  223.4 3.0 maximum_select_fusion.1
  226.4 55.2 %all-reduce.19.cloned.1.call-done = bf16[8,280,768]{2,1,0:T(8,128)(2,1)} async-done(((bf16[8,280,768]{2,1,0:T(8,128)(2,1)}), bf16[8,280,768]{2,1,0:T(8,128)(2,1)}) %all-reduce.19.cloned.1.call-update) | async-done | bytes 3440656 | tf_op jit(solution)/shard_map/psum | solution.py:125
  281.6 3.3 fusion.82
  287.6 18.2 %fusion.86 = (u8[280,1536]{1,0:T(8,128)(4,1)S(1)}, u8[280,1536]{1,0:T(8,128)(4,1)S(1)}, f32[8,280,1536]{2,1,0:T(8,128)}) fusion(f32[1536]{0:T(1024)} %convert_convert_fusion, bf16[384,1536]{1,0:T(8,128)(2,1)} %collective-permute-done.3, bf16[384,1536]{1,0:T(8,128)(2,1)} %maximum_select_fusion.1, pred[]{:T(512)S(6)} %eq.12, f32[768]{0:T(1024)} %convert_element_type.191, ...), kind=kOutput, calls=%fused_computation.134 | convolution fusion | flops 5358231552 | bytes 23896576 | tf_op jit(solution)/shard_map/psd,df->psf/dot_general | solution.py:129
  305.9 34.4 %multiply_convert_fusion.1 = (bf16[8,280,1536]{2,1,0:T(8,128)(2,1)}, f32[8,280,1536]{2,1,0:T(8,128)}) fusion(f32[8,280,1536]{2,1,0:T(8,128)} %get-tuple-element.187, f32[1536]{0:T(1024)S(1)} %copy-done.25, u8[280,1536]{1,0:T(8,128)(4,1)S(1)} %get-tuple-element.113, u8[280,1536]{1,0:T(8,128)(4,1)S(1)} %get-tuple-element.112), kind=kLoop, calls=%fused_computation.75 | loop fusion | flops 244285440 | bytes 35272704 | tf_op jit(solution)/shard_map/convert_element_type | solution.py:131
  340.3 18.5 %convert_reduce_fusion.1 = (f32[1536]{0:T(1024)}, bf16[8,280,1536]{2,1,0:T(8,128)(2,1)}) fusion(f32[8,280,1536]{2,1,0:T(8,128)} %get-tuple-element.173, bf16[1536,768]{0,1:T(8,128)(2,1)} %all-gather.5.cloned.1.call-done, bf16[8,280,768]{2,1,0:T(8,128)(2,1)} %param.21, f32[8,280]{1,0:T(8,128)} %fusion.109, f32[8,280,1536]{2,1,0:T(8,128)} %get-tuple-element.187, ...), kind=kOutput, calls=%fused_computation.73 | convolution fusion | flops 5348473344 | bytes 40227584 | tf_op jit(solution)/shard_map/psd,fd->psf/dot_general | solution.py:143
  358.8 11.4 %convolution_convert_fusion = bf16[8,280,768]{2,1,0:T(8,128)(2,1)} fusion(bf16[8,280,1536]{2,1,0:T(8,128)(2,1)} %get-tuple-element.189, bf16[384,1536]{1,0:T(8,128)(2,1)} %collective-permute-done.3, bf16[384,1536]{1,0:T(8,128)(2,1)} %maximum_select_fusion.1, pred[]{:T(512)S(6)} %eq.12), kind=kOutput, calls=%fused_computation.136 | convolution fusion | flops 5297160192 | bytes 12681217 | tf_op jit(solution)/shard_map/psf,df->psd/dot_general | solution.py:151
  370.3 9.9 convolution_convert_fusion.1
  380.2 82.5 %all-reduce.21.cloned.1.call-done = bf16[8,280,768]{2,1,0:T(8,128)(2,1)} async-done(((bf16[8,280,768]{2,1,0:T(8,128)(2,1)}), bf16[8,280,768]{2,1,0:T(8,128)(2,1)}) %all-reduce.21.cloned.1.call-update) | async-done | bytes 3440656 | tf_op jit(solution)/shard_map/psum | solution.py:150
  462.7 6.4 convert_reduce_fusion.3
  469.1 5.6 fusion.77
  474.7 4.9 fusion.114
  479.6 2.7 copy-done.3
  482.3 3.2 convolution_convert_fusion.3
  485.5 4.0 copy.62
  489.4 63.9 %while.23 = (s32[]{:T(128)}, bf16[4,2,280,3,6,64]{2,5,4,1,3,0:T(8,128)(2,1)}, bf16[4,2,280,6,64]{2,4,3,1,0:T(8,128)(2,1)}, f32[4,2,280]{2,1,0:T(2,128)}, bf16[4,...) while((s32[]{:T(128)}, ...), condition=%wide.region_15.16_spmd, body=%wide.region_13.15_spmd.sunk | while | flops 621167104 | bytes 36805476 | solution.py:190
  489.6 2.3 fusion.157
  492.7 3.4 multiply_reduce_fusion.3
  501.6 2.5 fusion.158
  508.6 3.4 multiply_reduce_fusion.3
  517.5 2.5 fusion.158
  521.5 2.3 fusion.157
  524.5 3.4 multiply_reduce_fusion.3
  533.4 2.5 fusion.158
  540.4 3.4 multiply_reduce_fusion.3
  549.3 2.5 fusion.158
  553.3 4.3 copy.63
  557.6 2.9 copy-done.6
  560.5 7.7 bitcast_convert_fusion
  568.6 7.4 fusion.102
  576.1 12.6 %convolution_bitcast_fusion.1 = f32[768,1536]{1,0:T(8,128)} fusion(bf16[8,280,1536]{2,1,0:T(8,128)(2,1)} %get-tuple-element.189, f32[768]{0:T(1024)S(1)} %copy-done.35, f32[768]{0:T(1024)S(1)} %copy-done.24, f32[8,280]{1,0:T(8,128)S(1)} %copy-done.20, f32[8,280]{1,0:T(8,128)S(1)} %broadcast_multiply_fusion, f32[768]{0:T(1024)S(1)} %convert_element_type.187, ...), kind=kOutput, calls=%fused_computation.130 | convolution fusion | flops 5300305920 | bytes 18508288 | tf_op jit(solution)/shard_map/psd,psf->df/dot_general | solution.py:149
  588.8 11.0 %convolution_bitcast_fusion = f32[1536,768]{0,1:T(8,128)} fusion(bf16[8,280,1536]{2,1,0:T(8,128)(2,1)} %get-tuple-element.172, bf16[8,280,768]{2,1,0:T(8,128)(2,1)} %param.21, f32[8,280]{1,0:T(8,128)S(1)} %copy-done.17), kind=kOutput, calls=%fused_computation.129 | convolution fusion | flops 5289984000 | bytes 15049472 | tf_op jit(solution)/shard_map/psf,psd->fd/dot_general | solution.py:140
  600.1 13.7 %convolution_bitcast_fusion.2 = f32[768,3,384]{2,0,1:T(8,128)} fusion(bf16[8,280,3,384]{1,3,2,0:T(8,128)(2,1)} %bitcast.169, bf16[8,280,768]{2,1,0:T(8,128)(2,1)S(1)} %copy-done, f32[768]{0:T(1024)S(1)} %copy-done.34, f32[768]{0:T(1024)S(1)} %copy-done.22, f32[8,280]{1,0:T(8,128)S(1)} %copy-done.15, f32[8,280]{1,0:T(8,128)S(1)} %copy-done.10), kind=kOutput, calls=%fused_computation.143 | convolution fusion | flops 3973939200 | bytes 12164608 | tf_op jit(solution)/shard_map/psd,pstc->dtc/dot_general | solution.py:204
  614.5 4.3 convert_reduce_fusion
  619.0 115.3 %all-reduce.23.cloned.1.call-done = (bf16[8,280,768]{2,1,0:T(8,128)(2,1)}, bf16[8,280,768]{2,1,0:T(8,128)(2,1)}) async-done(((bf16[8,280,768]{2,1,0:T(8,128)(2,1)}, bf16[8,280,768]{2,1,0:T(8,128)(2,1)}), (bf16[8,280,768]{2,1,0:T(8,128)(2,1)}, bf16[8,280,768]{2,1,0:T(8,128)(2,1)})) %all-reduce.23.cloned.1.call-update) | async-done | bytes 6881296 | tf_op jit(solution)/shard_map/psum | solution.py:133
  734.3 4.2 convert_reduce_fusion.2
  738.5 4.3 fusion.78
  742.9 61.8 %all-reduce.12 = (f32[768]{0:T(1024)S(1)}, f32[768]{0:T(1024)S(1)}, f32[2,384]{1,0:T(2,128)}, f32[768]{0:T(1024)}, f32[768]{0:T(1024)}, /*index=5*/f32[768]{0:T(1024)}, f32[1536]{0:T(1024)}, f32[768]{0:T(1024)S(1)}) all-reduce(f32[768]{0:T(1024)S(1)} %get-tuple-element.116, ...), channel_id=2, replica_groups=mesh['dp'=16,'mp'=2] {'dp'}, use_global_device_ids=true, to_apply=%region_20.21.clone | all-reduce | flops 6912 | bytes 55296
  810.2 11.0 %add_convert_fusion.1 = (bf16[8,280,768]{2,1,0:T(8,128)(2,1)}, bf16[8,280,768]{2,1,0:T(8,128)(2,1)}) fusion(f32[8,280,768]{2,1,0:T(8,128)} %copy-done.3, bf16[8,280,768]{2,1,0:T(8,128)(2,1)S(1)} %copy-done, bf16[8,280,768]{2,1,0:T(8,128)(2,1)} %get-tuple-element.169, f32[8,280]{1,0:T(8,128)S(1)} %negate_multiply_fusion.1, ...), kind=kLoop, calls=%fused_computation.116 | loop fusion | flops 32686080 | bytes 27579136 | tf_op jit(solution)/shard_map/convert_element_type | solution.py:212
  821.2 54.5 %reduce-scatter.9.cloned.1.call-done = f32[48,1536]{1,0:T(8,128)} async-done(((f32[768,1536]{1,0:T(8,128)}), f32[48,1536]{1,0:T(8,128)}) %reduce-scatter.9.cloned.1.call-update) | async-done | bytes 294928 | tf_op jit(solution)/shard_map/reduce_scatter | solution.py:217
  875.7 79.2 %reduce-scatter.11.cloned.1.call-done = f32[1536,48]{0,1:T(8,128)} async-done(((f32[1536,768]{0,1:T(8,128)}), f32[1536,48]{0,1:T(8,128)}) %reduce-scatter.11.cloned.1.call-update) | async-done | bytes 294928 | tf_op jit(solution)/shard_map/reduce_scatter | solution.py:218
  954.9 71.9 %reduce-scatter.5.cloned.1.call-done = f32[48,3,384]{2,0,1:T(8,128)} async-done(((f32[768,3,384]{2,0,1:T(8,128)}), f32[48,3,384]{2,0,1:T(8,128)}) %reduce-scatter.5.cloned.1.call-update) | async-done | bytes 221200 | tf_op jit(solution)/shard_map/reduce_scatter | solution.py:215
  (206 shorter events, 90.6 us)
Async XLA Ops:
  7.2 110.3 %copy-start = (bf16[8,280,768]{2,1,0:T(8,128)(2,1)S(1)}, bf16[8,280,768]{2,1,0:T(8,128)(2,1)}, u32[]{:S(2)}) copy-start(bf16[8,280,768]{2,1,0:T(8,128)(2,1)} %param.20) | copy-start | bytes 10321924
  7.2 110.3 %all-gather.3.cloned.1.call-start = ((), (), s32[]{:S(2)}) async-start(), calls=%async_computation.4 | async-start | bytes 1880064 | tf_op jit(solution)/shard_map/all_gather | solution.py:63
  9.0 272.5 %all-reduce.19.cloned.1.call-start = ((), (), s32[]{:S(2)}) async-start(), calls=%async_computation.5 | async-start | bytes 6881280 | tf_op jit(solution)/shard_map/psum | solution.py:125
  18.0 0.6 copy-start.33
  84.7 39.9 %copy-start.21 = (f32[768]{0:T(1024)}, f32[768]{0:T(1024)S(1)}, u32[]{:S(2)}) copy-start(f32[768]{0:T(1024)S(1)} %convert_element_type.172) | copy-start | bytes 9220
  88.7 1.6 copy-start.38
  92.9 31.7 %copy-start.9 = (f32[8,280]{1,0:T(8,128)}, f32[8,280]{1,0:T(8,128)S(1)}, u32[]{:S(2)}) copy-start(f32[8,280]{1,0:T(8,128)S(1)} %broadcast_multiply_fusion.1) | copy-start | bytes 26884
  96.0 0.6 copy-start.11
  135.0 9.5 copy-start.28
  135.0 9.5 copy-start.29
  184.5 27.4 %copy-start.37 = (bf16[768]{0:T(1024)(128)(2,1)S(1)}, bf16[768]{0:T(1024)(128)(2,1)}, u32[]{:S(2)}) copy-start(bf16[768]{0:T(1024)(128)(2,1)} %get-tuple-element.162) | copy-start | bytes 4612
  184.5 29.3 %copy-start.32 = (f32[1536]{0:T(1024)S(1)}, f32[1536]{0:T(1024)}, u32[]{:S(2)}) copy-start(f32[1536]{0:T(1024)} %param.31) | copy-start | bytes 18436
  190.5 149.9 %all-gather.5.cloned.1.call-start = ((), (), s32[]{:S(2)}) async-start(), calls=%async_computation.6 | async-start | bytes 2506752 | tf_op jit(solution)/shard_map/all_gather | solution.py:66
  192.2 1.7 collective-permute-start
  196.1 9.8 collective-permute-start.1
  208.2 15.3 %collective-permute-start.2 = (bf16[192,1536]{1,0:T(8,128)(2,1)}, bf16[192,1536]{1,0:T(8,128)(2,1)}, u32[]{:S(2)}, u32[]{:S(2)}) collective-permute-start(bf16[192,1536]{1,0:T(8,128)(2,1)} %maximum_select_fusion.2), channel_id=1, source_target_pairs={{0,8},{2,10},{4,12},{6,14},{8,0},{10,2},{12,4},{14,6},{16,24},{18,... | collective-permute-start | bytes 1769480 | tf_op jit(solution)/shard_map/ppermute | solution.py:46
  209.8 252.8 %all-reduce.21.cloned.1.call-start = ((), (), s32[]{:S(2)}) async-start(), calls=%async_computation.7 | async-start | bytes 6881280 | tf_op jit(solution)/shard_map/psum | solution.py:150
  226.4 61.2 %collective-permute-start.3 = (bf16[384,1536]{1,0:T(8,128)(2,1)}, bf16[384,1536]{1,0:T(8,128)(2,1)}, u32[]{:S(2)}, u32[]{:S(2)}) collective-permute-start(bf16[384,1536]{1,0:T(8,128)(2,1)} %maximum_select_fusion.1), channel_id=1, source_target_pairs={{0,16},{2,18},{4,20},{6,22},{8,24},{10,26},{12,28},{14,30},{16,0},... | collective-permute-start | bytes 3538952 | tf_op jit(solution)/shard_map/ppermute | solution.py:46
  281.6 3.3 copy-start.1
  287.0 0.6 copy-start.13
  287.6 18.2 %copy-start.18 = (f32[8,280]{1,0:T(8,128)}, f32[8,280]{1,0:T(8,128)S(1)}, u32[]{:S(2)}) copy-start(f32[8,280]{1,0:T(8,128)S(1)} %fusion.111) | copy-start | bytes 26884
  287.6 18.2 %copy-start.25 = (f32[1536]{0:T(1024)S(1)}, f32[1536]{0:T(1024)}, u32[]{:S(2)}) copy-start(f32[1536]{0:T(1024)} %convert_convert_fusion) | copy-start | bytes 18436
  370.2 364.1 %all-reduce.23.cloned.1.call-start = ((), (), s32[]{:S(2)}) async-start(), calls=%async_computation.12 | async-start | bytes 13762560 | tf_op jit(solution)/shard_map/psum | solution.py:133
  462.7 6.4 copy-start.14
  462.7 6.4 copy-start.2
  462.7 6.4 copy-start.5
  462.7 6.4 copy-start.19
  462.7 6.4 copy-start.23
  469.0 5.6 copy-start.7
  469.0 5.6 copy-start.16
  474.7 7.6 copy-start.8
  479.5 2.8 copy-start.3
  553.3 7.2 copy-start.39
  557.5 2.9 copy-start.6
  568.2 7.9 copy-start.20
  568.2 7.9 copy-start.24
  568.2 7.9 copy-start.35
  568.2 253.0 %reduce-scatter.7.cloned.1.call-start = ((), (), s32[]{:S(2)}) async-start(), calls=%async_computation.9 | async-start | bytes 1253376 | tf_op jit(solution)/shard_map/reduce_scatter | solution.py:216
  576.0 12.8 %copy-start.17 = (f32[8,280]{1,0:T(8,128)S(1)}, f32[8,280]{1,0:T(8,128)}, u32[]{:S(2)}) copy-start(f32[8,280]{1,0:T(8,128)} %fusion.109) | copy-start | bytes 26884
  576.0 299.7 %reduce-scatter.9.cloned.1.call-start = ((), (), s32[]{:S(2)}) async-start(), calls=%async_computation.10 | async-start | bytes 5013504 | tf_op jit(solution)/shard_map/reduce_scatter | solution.py:217
  588.7 11.4 %copy-start.10 = (f32[8,280]{1,0:T(8,128)S(1)}, f32[8,280]{1,0:T(8,128)}, u32[]{:S(2)}) copy-start(f32[8,280]{1,0:T(8,128)} %copy-done.9) | copy-start | bytes 26884
  588.7 11.4 %copy-start.15 = (f32[8,280]{1,0:T(8,128)S(1)}, f32[8,280]{1,0:T(8,128)}, u32[]{:S(2)}) copy-start(f32[8,280]{1,0:T(8,128)} %fusion.110) | copy-start | bytes 26884
  588.7 11.4 %copy-start.22 = (f32[768]{0:T(1024)S(1)}, f32[768]{0:T(1024)}, u32[]{:S(2)}) copy-start(f32[768]{0:T(1024)} %copy-done.21) | copy-start | bytes 9220
  588.7 11.4 %copy-start.34 = (f32[768]{0:T(1024)S(1)}, f32[768]{0:T(1024)}, u32[]{:S(2)}) copy-start(f32[768]{0:T(1024)} %convert_element_type.174) | copy-start | bytes 9220
  588.7 366.2 %reduce-scatter.11.cloned.1.call-start = ((), (), s32[]{:S(2)}) async-start(), calls=%async_computation.11 | async-start | bytes 5013504 | tf_op jit(solution)/shard_map/reduce_scatter | solution.py:218
  599.8 14.0 %copy-start.36 = (bf16[768]{0:T(1024)(128)(2,1)S(1)}, bf16[768]{0:T(1024)(128)(2,1)}, u32[]{:S(2)}) copy-start(bf16[768]{0:T(1024)(128)(2,1)} %get-tuple-element.167) | copy-start | bytes 4612
  599.8 426.9 %reduce-scatter.5.cloned.1.call-start = ((), (), s32[]{:S(2)}) async-start(), calls=%async_computation.8 | async-start | bytes 3760128 | tf_op jit(solution)/shard_map/reduce_scatter | solution.py:215
  614.5 124.0 %copy-start.12 = (f32[8,280]{1,0:T(8,128)S(1)}, f32[8,280]{1,0:T(8,128)}, u32[]{:S(2)}) copy-start(f32[8,280]{1,0:T(8,128)} %copy-done.11) | copy-start | bytes 26884
  734.3 4.2 copy-start.4
  734.3 8.5 copy-start.26
  734.3 8.5 copy-start.27
  734.3 8.5 copy-start.30
  734.3 8.5 copy-start.31
Sparse Core Ops, SparseCore 0:
  10.9 43.1 all-gather.2
  190.6 90.9 all-reduce.18
  284.4 42.3 all-gather.4
  370.4 92.2 all-reduce.20
  568.3 165.9 all-reduce.22
  738.4 58.2 reduce-scatter.6
  801.0 74.6 reduce-scatter.8
  880.1 74.7 reduce-scatter.10
  959.4 67.3 reduce-scatter.4
